TPU v7x, 256 devices: a whole 4x4x8 slice. The times are simulated.
256 devices in a mesh: row: 32 (over x, z_hi, y), col: 8 (over z_lo, core).
Axes of the slice: x: 4, y: 4, z: 8 (z_hi: 2, z_lo: 4; z = z_hi * 4 + z_lo), core: 2. Of those that a mesh axis runs over, the one named last changes fastest.
Arguments:
- green: bfloat16 [2, 2048, 16384], P(None, 'col', 'row'), may hold values from -6 to 6
- step_sigma: bfloat16 [2, 2048, 256], P(None, 'col'), may hold values from -0.21875 to 0.21875
- hist_sigma: bfloat16 [2, 4, 2048, 1024], P(None, None, 'col', 'row'), may hold values from -0.1875 to 0.1875
- green_hist: bfloat16 [2, 1792, 16384], P(None, None, 'row'), may hold values from -6 to 6
- resident: bfloat16 [2, 2048, 16384], P(None, 'col', 'row'), may hold values from -0.1875 to 0.1875
Outputs:
- green_out: bfloat16 [2, 2048, 16384], P(None, 'col', 'row')
- mirror_out: bfloat16 [2, 2048, 8192], P(None, 'col', 'row')
All inputs are finite; a program needn't handle non-finite values.
Results may differ from a plain program's by a relative error of at most 0.014.
Values may be sent and summed in bfloat16 or wider, within the bound.
No kernel may reach another device: no remote copies, remote signals or barrier semaphores. Data moves between devices by JAX's collectives and lax.ppermute only.
A program may use at most 64 MiB of HBM per device.

v0:
```python
import functools

import jax
import jax.numpy as jnp
from jax import lax
from jax.experimental import pallas as pl
from jax.experimental.pallas import tpu as pltpu
from jax.sharding import PartitionSpec as P


TB = 256
CHUNKS = 2
SHIFTS = (1, -1, 2)
OFFSETS = (0, -1, 1, 2)
BATCHES = ((0, 2), (2, 4))
PARTS = (((0, 1), (1, 2)), ((2, 4),))
WIDE = TB // CHUNKS
HW = 4
TICKS = 4
TIME_STEP = 0.2
BOTH = ("row", "col")
F32 = jnp.float32
BF16 = jnp.bfloat16


VMEM = pl.BlockSpec(memory_space=pltpu.VMEM)


def pairs_of(move):
    pairs = []
    for row in range(32):
        for col in range(8):
            there = move(row // 8, (row // 4) % 2, row % 4, col // 2, col % 2)
            x, high, y, chip, core = there
            pairs.append((row * 8 + col, (x * 8 + high * 4 + y) * 8 + chip * 2 + core))
    return pairs


def send(value, move):
    return lax.ppermute(value, BOTH, pairs_of(move))


def early_axis(by):
    def move(x, high, y, chip, core):
        return (x, high, (y + by) % 4, chip, core) if core == 0 else ((x + by) % 4, high, y, chip, core)

    return move


def late_axis(by):
    def move(x, high, y, chip, core):
        return ((x + by) % 4, high, y, chip, core) if core == 0 else (x, high, (y + by) % 4, chip, core)

    return move


def other_high(x, high, y, chip, core):
    return x, high ^ 1, y, chip, core


def other_core(x, high, y, chip, core):
    return x, high, y, chip, core ^ 1


def other_branch(x, high, y, chip, core):
    return x ^ 2, high, y, chip, core


def next_chip(step):
    first = max(step - (TICKS - 1), 0)
    last = min(step, 2) + 1

    def move(x, high, y, chip, core):
        if first <= chip < last:
            return x, high, y, chip + 1, core
        if chip == last:
            return x, high, y, first, core
        return x, high, y, chip, core ^ 1

    return move


def call(kernel, outs, scratch, flops, moved, *args):
    specs = [VMEM] * len(args)
    return pl.pallas_call(
        kernel,
        out_shape=outs,
        in_specs=specs,
        out_specs=jax.tree.map(lambda _: VMEM, outs),
        scratch_shapes=scratch,
        compiler_params=pltpu.CompilerParams(vmem_limit_bytes=24 << 20),
        cost_estimate=pl.CostEstimate(flops=flops, bytes_accessed=moved, transcendentals=0),
    )(*args)


def dot(left, right):
    return jnp.dot(left, right, preferred_element_type=F32)


def complex_dot(left_real, left_imag, right_real, right_imag):
    real_part = dot(left_real, right_real) - dot(left_imag, right_imag)
    imag_part = dot(left_real, right_imag) + dot(left_imag, right_real)
    return real_part, imag_part


def shape(dims, dtype):
    return jax.ShapeDtypeStruct(dims, dtype)


def place():
    row = lax.axis_index("row")
    col = lax.axis_index("col")
    return row // 8, (row // 4) % 2, row % 4, col // 2, col % 2


def load_kernel(mine_ref, out_ref):
    out_ref[...] = mine_ref[...]


def split_kernel(start, mine_ref, theirs_ref, out_ref):
    for at in range(out_ref.shape[0]):
        for part in range(2):
            out_ref[at, 0, part] = mine_ref[part, start + at]
            out_ref[at, 1, part] = theirs_ref[part, at]


def join_kernel(start, stop, *refs):
    out_ref = refs[-1]
    for slot, from_ref in enumerate(refs[:-1]):
        out_ref[slot] = from_ref[start:stop]


def pack_kernel(sigma_ref, green_ref, out_ref, own_ref):
    core = place()[4]
    out_ref[0:2] = sigma_ref[...]
    out_ref[2:4] = green_ref[:, :, pl.ds(pl.multiple_of((1 - core) * TB, TB), TB)]
    own_ref[...] = green_ref[:, :, pl.ds(pl.multiple_of(core * TB, TB), TB)]


def prepare_kernel(packed_ref, own_ref, swapped_ref, even_ref, odd_ref, both_ref, state_ref, base_ref, link_ref):
    core = place()[4]
    first = core == 0
    own = own_ref[...]
    even_ref[...] = jnp.where(first, packed_ref[0:2], swapped_ref[0:2])
    odd_ref[...] = jnp.where(first, swapped_ref[0:2], packed_ref[0:2])
    state_ref[0] = jnp.where(first, own, swapped_ref[2:4])
    state_ref[1] = jnp.where(first, swapped_ref[2:4], own)
    real_part, imag_part = complex_dot(odd_ref[0], odd_ref[1], even_ref[0], even_ref[1])
    both_ref[0] = real_part.astype(BF16)
    both_ref[1] = imag_part.astype(BF16)
    set_base(odd_ref, state_ref, base_ref)
    for half in range(CHUNKS):
        put_link(link_ref.at[half], base_ref, half)


def put_link(link_ref, base_ref, half):
    columns = slice(half * WIDE, (half + 1) * WIDE)
    link_ref[:, :WIDE] = base_ref[0, :, columns].astype(BF16)
    link_ref[:, WIDE:] = base_ref[1, :, columns].astype(BF16)


def set_base(odd_ref, state_ref, base_ref):
    real_part, imag_part = complex_dot(odd_ref[0], odd_ref[1], state_ref[0, 0], state_ref[0, 1])
    base_ref[0] = real_part + state_ref[1, 0].astype(F32)
    base_ref[1] = imag_part + state_ref[1, 1].astype(F32)


def turned(left, right):
    return lax.dot_general(left, right, (((0,), (0,)), ((), ())), preferred_element_type=F32)


def put_history(tick, side, real_ref, imag_ref, past_ref, out_ref):
    rows = slice(tick * TB, (tick + HW) * TB)
    at = pl.ds(pl.multiple_of(side * TB, TB), TB)

    @pl.loop(0, 2)
    def _(part):
        by_imag = turned(imag_ref[...], past_ref[1 - part, rows, at])
        by_imag = jnp.where(part == 0, -by_imag, by_imag)
        out_ref[part] = (turned(real_ref[...], past_ref[part, rows, at]) + by_imag).astype(BF16)


def keep_kernel(tick, real_ref, imag_ref, past_ref, out_ref):
    put_history(tick, place()[4], real_ref, imag_ref, past_ref, out_ref)


def history_kernel(tick, stacked, *refs):
    sigma_refs = refs[:4]
    past_ref, give_ref, real_ref, imag_ref = refs[4:]
    x, high, y, _, core = place()
    upright = core == 0
    for outer in range(4):
        for inner in range(4):
            x_at = (x + jnp.where(upright, OFFSETS[outer], OFFSETS[inner]) + 4) % 4
            y_at = (y + jnp.where(upright, OFFSETS[inner], OFFSETS[outer]) + 4) % 4
            for deep in range(2):
                at = pl.ds(pl.multiple_of((x_at * 8 + (high ^ deep) * 4 + y_at) * 32, 32), 32)
                real_ref[at, :] = sigma_refs[outer][inner, stacked, deep, 0]
                imag_ref[at, :] = sigma_refs[outer][inner, stacked, deep, 1]

    put_history(tick, 1 - core, real_ref, imag_ref, past_ref, give_ref)


def link_kernel(half, early, both_ref, carry_ref, base_ref, out_ref):
    chip = place()[3]

    @pl.when(chip == 0)
    def _():
        put_link(out_ref, base_ref, half)

    @pl.when(chip > 0)
    def _():
        carry = carry_ref[half] if early else carry_ref[...]
        columns = slice(half * WIDE, (half + 1) * WIDE)
        by_real = dot(both_ref[0], carry)
        by_imag = dot(both_ref[1], carry)
        out_ref[:, :WIDE] = (by_real[:, :WIDE] - by_imag[:, WIDE:] + base_ref[0, :, columns]).astype(BF16)
        out_ref[:, WIDE:] = (by_real[:, WIDE:] + by_imag[:, :WIDE] + base_ref[1, :, columns]).astype(BF16)


def update_kernel(step, ticks, n_carry, *refs):
    refs = list(refs)
    last = step == 6
    even_ref, odd_ref, state_ref, base_ref = refs[:4]
    carry_refs = refs[4 : 4 + n_carry]
    refs = refs[4 + n_carry :]
    pasts = [(refs.pop(0), refs.pop(0)) for _ in ticks]
    out_ref, other_ref, past_ref = refs
    _, _, _, chip, core = place()
    valid = (chip <= step) & (chip >= step - (TICKS - 1))

    def copy_past(keep_ref, swap_ref):
        first = core == 0
        past_ref[0] = jnp.where(first, keep_ref[...], swap_ref[...])
        past_ref[1] = jnp.where(first, swap_ref[...], keep_ref[...])

    @pl.when(valid)
    def _():
        for tick, (keep_ref, swap_ref) in zip(ticks, pasts):
            pl.when(chip == step - tick)(functools.partial(copy_past, keep_ref, swap_ref))
        state = [[state_ref[block, part].astype(F32) for part in range(2)] for block in range(2)]
        even_carry = [jnp.zeros((TB, TB), F32)] * 2
        odd_carry = state[0]
        if n_carry:
            inside = chip > 0
            halves = [carry_refs[0][half] for half in range(CHUNKS)] if step == 1 else [ref[...] for ref in carry_refs]
            carry = [
                jnp.concatenate([half[:, part * WIDE : (part + 1) * WIDE] for half in halves], axis=1)
                for part in range(2)
            ]
            carry = [jnp.where(inside, part, jnp.zeros((TB, TB), BF16)) for part in carry]
            even_carry = [part.astype(F32) for part in carry]
            moved = complex_dot(even_ref[0], even_ref[1], carry[0], carry[1])
            odd_carry = [moved[part] + state[0][part] for part in range(2)]
        carries = (even_carry, odd_carry)
        new_ref = past_ref if last else out_ref
        for block in range(2):
            past = [past_ref[block, part].astype(F32) for part in range(2)]
            new_real = state[block][0] + TIME_STEP * (past[1] + carries[block][1])
            new_imag = state[block][1] - TIME_STEP * (past[0] + carries[block][0])
            new_ref[block, 0] = new_real.astype(BF16)
            new_ref[block, 1] = new_imag.astype(BF16)
        if not last:
            set_base(odd_ref, out_ref, other_ref)

    @pl.when(jnp.logical_not(valid))
    def _():
        if last:
            past_ref[...] = state_ref[...]
        else:
            out_ref[...] = state_ref[...]
            other_ref[...] = base_ref[...]

    if last:
        first = core == 0
        out_ref[...] = jnp.where(first, past_ref[0], past_ref[1])
        other_ref[...] = jnp.where(first, past_ref[1], past_ref[0])


def mirror_kernel(resident_ref, keep_ref, swap_ref, out_ref):
    core = place()[4]

    def across(left, right):
        return lax.dot_general(left, right, (((1,), (1,)), ((), ())), preferred_element_type=F32)

    real_part = jnp.zeros((TB, TB), F32)
    imag_part = jnp.zeros((TB, TB), F32)
    for green_ref, side in ((keep_ref, core), (swap_ref, 1 - core)):
        at = pl.ds(pl.multiple_of(side * TB, TB), TB)
        held_real, held_imag = resident_ref[0, :, at], resident_ref[1, :, at]
        real_part += across(held_real, green_ref[0]) + across(held_imag, green_ref[1])
        imag_part += across(held_imag, green_ref[0]) - across(held_real, green_ref[1])
    out_ref[0] = real_part.astype(BF16)
    out_ref[1] = imag_part.astype(BF16)


def steps(green, step_sigma, hist_sigma, green_hist, resident):
    core = lax.axis_index("col") % 2
    square = (2, TB, TB)
    unit = 8 * TB**3
    pair = (shape(square, BF16), shape(square, BF16))
    state_shape = (shape((2, *square), BF16), shape(square, F32))

    mine = jnp.swapaxes(hist_sigma, 2, 3)
    theirs = [send(mine[:, start:stop], other_high) for start, stop in BATCHES]
    loaded = call(load_kernel, shape(mine.shape, BF16), [], TB, 1 << 18, mine)

    packed, own_green = call(
        pack_kernel, (shape((4, TB, TB), BF16), shape(square, BF16)), [], TB, 1 << 20, step_sigma, green
    )
    swapped = send(packed, other_core)
    partner_resident = send(resident, other_branch)
    even, odd, both, state, base, link = call(
        prepare_kernel, (shape(square, BF16), *pair, *state_shape, shape((CHUNKS, TB, 2 * WIDE), BF16)),
        [], 2 * unit, 4 << 20, packed, own_green, swapped,
    )
    carries = [send(link, next_chip(0))]

    pasts = []
    for batch, (start, stop) in enumerate(BATCHES):
        own = call(
            functools.partial(split_kernel, start),
            shape((stop - start, 2, 2, 32, TB), BF16), [], TB, 1 << 19, loaded, theirs[batch],
        )
        near = [own] + [send(own, early_axis(by)) for by in SHIFTS]
        for first, end in PARTS[batch]:
            block = call(
                functools.partial(join_kernel, first - start, end - start),
                shape((4, end - first, 2, 2, 32, TB), BF16), [], TB, 1 << 20, *near,
            )
            far = [send(block, late_axis(by)) for by in SHIFTS]
            for tick in range(first, end):
                table = shape((HW * TB, TB), BF16)
                give, real, imag = call(
                    functools.partial(history_kernel, tick, tick - first),
                    (shape(square, BF16), table, table), [], 4 * unit, 4 << 20, block, *far, green_hist,
                )
                traded = send(give, other_core)
                keep = call(
                    functools.partial(keep_kernel, tick),
                    shape(square, BF16), [], 4 * unit, 3 << 20, real, imag, green_hist,
                )
                pasts.append((keep, traded))

    for step in range(7):
        new_carries = carries
        if 0 < step < 6:
            new_carries = []
            for half in range(CHUNKS):
                early = step == 1
                link = call(
                    functools.partial(link_kernel, half, early),
                    shape((TB, 2 * WIDE), BF16), [], unit, 1 << 19, both, carries[0 if early else half], base,
                )
                new_carries.append(send(link, next_chip(step)))
        ticks = [step - chip for chip in range(4) if 0 <= step - chip < TICKS]
        used = carries if step else []
        args = [even, odd, state, base, *used]
        for tick in ticks:
            args.extend(pasts[tick])
        state, base = call(
            functools.partial(update_kernel, step, ticks, len(used)),
            pair if step == 6 else state_shape, [pltpu.VMEM((2, *square), BF16)], 2 * unit, 4 << 20, *args,
        )
        carries = new_carries

    keep, give = state, base
    got = send(give, other_core)
    mirrored = call(mirror_kernel, shape(square, BF16), [], 2 * unit, 2 << 20, partner_resident, keep, got)
    mirror_out = send(mirrored, other_branch)
    green_out = jnp.where(core == 0, jnp.concatenate([keep, got], axis=2), jnp.concatenate([got, keep], axis=2))
    return green_out, mirror_out


def solution(mesh):
    placed = (
        P(None, "col", "row"),
        P(None, "col", None),
        P(None, None, "col", "row"),
        P(None, None, "row"),
        P(None, "col", "row"),
    )
    return jax.shard_map(
        steps,
        mesh=mesh,
        in_specs=placed,
        out_specs=(P(None, "col", "row"), P(None, "col", "row")),
        check_vma=False,
    )
```

profile of v0, /device:TPU:2, one launch (start us, length us, event | category | flops | bytes accessed | tf_op | source)
XLA Modules:
  0.0 123.3 jit_solution(4954335949776803626)
XLA Ops:
  1.7 7.3 %collective-permute-start.1 = (bf16[2,2,32,256]{3,2,1,0:T(8,128)(2,1)S(1)}, bf16[2,2,32,256]{3,2,1,0:T(8,128)(2,1)S(1)}, u32[]{:S(2)}, u32[]{:S(2)}) collective-permute-start(bf16[2,2,32,256]{3,2,1,0:T(8,128)(2,1)S(1)} %get-tuple-element.71), channel_id=1, source_target_pairs={{0,32},{1,33},{2,34},{3,35},{4,36},{5,37},{6,38},{7,39},{8,40},{9,... | collective-permute-start | bytes 196616 | tf_op jit(solution)/shard_map/ppermute | solution.py:40
  9.9 1.5 %collective-permute-done.1.theirs_ref = bf16[2,2,32,256]{3,2,1,0:T(8,128)(2,1)S(1)} collective-permute-done((bf16[2,2,32,256]{3,2,1,0:T(8,128)(2,1)S(1)}, bf16[2,2,32,256]{3,2,1,0:T(8,128)(2,1)S(1)}, u32[]{:S(2)}, u32[]{:S(2)}) %collective-permute-start.1) | collective-permute-done | bytes 65568 | tf_op jit(solution)/shard_map/ppermute | solution.py:40
  11.4 1.7 %collective-permute-start.2 = (bf16[2,2,2,32,256]{4,3,2,1,0:T(8,128)(2,1)S(1)}, bf16[2,2,2,32,256]{4,3,2,1,0:T(8,128)(2,1)S(1)}, u32[]{:S(2)}, u32[]{:S(2)}) collective-permute-start(bf16[2,2,2,32,256]{4,3,2,1,0:T(8,128)(2,1)S(1)} %shard_map.71.refs_0_), channel_id=1, source_target_pairs={{0,8},{1,65},{2,10},{3,67},{4,12},{5,69},{6,14},{7,71},{8,16},{9,7... | collective-permute-start | bytes 393224 | tf_op jit(solution)/shard_map/ppermute | solution.py:40
  13.1 1.7 %collective-permute-start.3 = (bf16[2,2,2,32,256]{4,3,2,1,0:T(8,128)(2,1)S(1)}, bf16[2,2,2,32,256]{4,3,2,1,0:T(8,128)(2,1)S(1)}, u32[]{:S(2)}, u32[]{:S(2)}) collective-permute-start(bf16[2,2,2,32,256]{4,3,2,1,0:T(8,128)(2,1)S(1)} %shard_map.71.refs_0_), channel_id=1, source_target_pairs={{0,24},{1,193},{2,26},{3,195},{4,28},{5,197},{6,30},{7,199},{8,0},... | collective-permute-start | bytes 393224 | tf_op jit(solution)/shard_map/ppermute | solution.py:40
  14.7 2.0 %collective-permute-start.4 = (bf16[2,2,2,32,256]{4,3,2,1,0:T(8,128)(2,1)S(1)}, bf16[2,2,2,32,256]{4,3,2,1,0:T(8,128)(2,1)S(1)}, u32[]{:S(2)}, u32[]{:S(2)}) collective-permute-start(bf16[2,2,2,32,256]{4,3,2,1,0:T(8,128)(2,1)S(1)} %shard_map.71.refs_0_), channel_id=1, source_target_pairs={{0,16},{1,129},{2,18},{3,131},{4,20},{5,133},{6,22},{7,135},{8,24}... | collective-permute-start | bytes 393224 | tf_op jit(solution)/shard_map/ppermute | solution.py:40
  16.7 6.4 %collective-permute-start.16 = (bf16[2,2,32,256]{3,2,1,0:T(8,128)(2,1)S(1)}, bf16[2,2,32,256]{3,2,1,0:T(8,128)(2,1)S(1)}, u32[]{:S(2)}, u32[]{:S(2)}) collective-permute-start(bf16[2,2,32,256]{3,2,1,0:T(8,128)(2,1)S(1)} %get-tuple-element.70), channel_id=1, source_target_pairs={{0,32},{1,33},{2,34},{3,35},{4,36},{5,37},{6,38},{7,39},{8,40},{9,... | collective-permute-start | bytes 196616 | tf_op jit(solution)/shard_map/ppermute | solution.py:40
  23.1 1.6 %collective-permute-start.5 = (bf16[4,1,2,2,32,256]{5,4,3,2,1,0:T(8,128)(2,1)S(1)}, bf16[4,1,2,2,32,256]{5,4,3,2,1,0:T(8,128)(2,1)S(1)}, u32[]{:S(2)}, u32[]{:S(2)}) collective-permute-start(bf16[4,1,2,2,32,256]{5,4,3,2,1,0:T(8,128)(2,1)S(1)} %shard_map.72.refs_0_), channel_id=1, source_target_pairs={{0,64},{1,9},{2,66},{3,11},{4,68},{5,13},{6,70},{7,15},{8,72},{9,1... | collective-permute-start | bytes 786440 | tf_op jit(solution)/shard_map/ppermute | solution.py:40
  26.8 2.3 %collective-permute-start.18 = (bf16[2,2,2,32,256]{4,3,2,1,0:T(8,128)(2,1)S(1)}, bf16[2,2,2,32,256]{4,3,2,1,0:T(8,128)(2,1)S(1)}, u32[]{:S(2)}, u32[]{:S(2)}) collective-permute-start(bf16[2,2,2,32,256]{4,3,2,1,0:T(8,128)(2,1)S(1)} %shard_map.82.refs_0_), channel_id=1, source_target_pairs={{0,24},{1,193},{2,26},{3,195},{4,28},{5,197},{6,30},{7,199},{8,0},... | collective-permute-start | bytes 393224 | tf_op jit(solution)/shard_map/ppermute | solution.py:40
  29.9 7.4 %collective-permute-done.17.refs_1_ = bf16[2,2,2,32,256]{4,3,2,1,0:T(8,128)(2,1)S(1)} collective-permute-done((bf16[2,2,2,32,256]{4,3,2,1,0:T(8,128)(2,1)S(1)}, bf16[2,2,2,32,256]{4,3,2,1,0:T(8,128)(2,1)S(1)}, u32[]{:S(2)}, u32[]{:S(2)}) %collective-permute-start.17) | collective-permute-done | bytes 131104 | tf_op jit(solution)/shard_map/ppermute | solution.py:40
  40.7 2.1 %collective-permute-start.11 = (bf16[4,1,2,2,32,256]{5,4,3,2,1,0:T(8,128)(2,1)S(1)}, bf16[4,1,2,2,32,256]{5,4,3,2,1,0:T(8,128)(2,1)S(1)}, u32[]{:S(2)}, u32[]{:S(2)}) collective-permute-start(bf16[4,1,2,2,32,256]{5,4,3,2,1,0:T(8,128)(2,1)S(1)} %shard_map.76.refs_0_), channel_id=1, source_target_pairs={{0,192},{1,25},{2,194},{3,27},{4,196},{5,29},{6,198},{7,31},{8,200... | collective-permute-start | bytes 786440 | tf_op jit(solution)/shard_map/ppermute | solution.py:40
  43.8 1.4 %collective-permute-done.7.refs_3_ = bf16[4,1,2,2,32,256]{5,4,3,2,1,0:T(8,128)(2,1)S(1)} collective-permute-done((bf16[4,1,2,2,32,256]{5,4,3,2,1,0:T(8,128)(2,1)S(1)}, bf16[4,1,2,2,32,256]{5,4,3,2,1,0:T(8,128)(2,1)S(1)}, u32[]{:S(2)}, u32[]{:S(2)}) %collective-permute-start.7) | collective-permute-done | bytes 262176 | tf_op jit(solution)/shard_map/ppermute | solution.py:40
  48.0 3.2 %collective-permute-start.12 = (bf16[4,1,2,2,32,256]{5,4,3,2,1,0:T(8,128)(2,1)S(1)}, bf16[4,1,2,2,32,256]{5,4,3,2,1,0:T(8,128)(2,1)S(1)}, u32[]{:S(2)}, u32[]{:S(2)}) collective-permute-start(bf16[4,1,2,2,32,256]{5,4,3,2,1,0:T(8,128)(2,1)S(1)} %shard_map.76.refs_0_), channel_id=1, source_target_pairs={{0,128},{1,17},{2,130},{3,19},{4,132},{5,21},{6,134},{7,23},{8,136... | collective-permute-start | bytes 786440 | tf_op jit(solution)/shard_map/ppermute | solution.py:40
  52.9 10.6 %collective-permute-done.12.refs_3_ = bf16[4,1,2,2,32,256]{5,4,3,2,1,0:T(8,128)(2,1)S(1)} collective-permute-done((bf16[4,1,2,2,32,256]{5,4,3,2,1,0:T(8,128)(2,1)S(1)}, bf16[4,1,2,2,32,256]{5,4,3,2,1,0:T(8,128)(2,1)S(1)}, u32[]{:S(2)}, u32[]{:S(2)}) %collective-permute-start.12) | collective-permute-done | bytes 262176 | tf_op jit(solution)/shard_map/ppermute | solution.py:40
  63.5 2.3 %collective-permute-start.9 = (bf16[2,256,256]{2,1,0:T(8,128)(2,1)S(1)}, bf16[2,256,256]{2,1,0:T(8,128)(2,1)S(1)}, u32[]{:S(2)}, u32[]{:S(2)}) collective-permute-start(bf16[2,256,256]{2,1,0:T(8,128)(2,1)S(1)} %get-tuple-element.47), channel_id=1, source_target_pairs={{0,2},{1,3},{2,0},{3,1},{4,5},{5,4},{6,7},{7,6},{8,10},{9,11},{10,... | collective-permute-start | bytes 786440 | tf_op jit(solution)/shard_map/ppermute | solution.py:40
  70.2 2.3 %collective-permute-start.14 = (bf16[256,256]{1,0:T(8,128)(2,1)S(1)}, bf16[256,256]{1,0:T(8,128)(2,1)S(1)}, u32[]{:S(2)}, u32[]{:S(2)}) collective-permute-start(bf16[256,256]{1,0:T(8,128)(2,1)S(1)} %shard_map.80), channel_id=1, source_target_pairs={{0,2},{1,3},{2,4},{3,5},{4,0},{5,1},{6,7},{7,6},{8,10},{9,11},{10,... | collective-permute-start | bytes 393224 | tf_op jit(solution)/shard_map/ppermute | solution.py:40
  75.6 1.9 %collective-permute-done.14.refs_4_.carry_ref = bf16[256,256]{1,0:T(8,128)(2,1)S(1)} collective-permute-done((bf16[256,256]{1,0:T(8,128)(2,1)S(1)}, bf16[256,256]{1,0:T(8,128)(2,1)S(1)}, u32[]{:S(2)}, u32[]{:S(2)}) %collective-permute-start.14) | collective-permute-done | bytes 131104 | tf_op jit(solution)/shard_map/ppermute | solution.py:40
  81.5 4.2 %collective-permute-done.24.refs_4_.carry_ref = bf16[256,256]{1,0:T(8,128)(2,1)S(1)} collective-permute-done((bf16[256,256]{1,0:T(8,128)(2,1)S(1)}, bf16[256,256]{1,0:T(8,128)(2,1)S(1)}, u32[]{:S(2)}, u32[]{:S(2)}) %collective-permute-start.24) | collective-permute-done | bytes 131104 | tf_op jit(solution)/shard_map/ppermute | solution.py:40
  85.8 2.3 %collective-permute-done.25.refs_5_.carry_ref = bf16[256,256]{1,0:T(8,128)(2,1)S(1)} collective-permute-done((bf16[256,256]{1,0:T(8,128)(2,1)S(1)}, bf16[256,256]{1,0:T(8,128)(2,1)S(1)}, u32[]{:S(2)}, u32[]{:S(2)}) %collective-permute-start.25) | collective-permute-done | bytes 131104 | tf_op jit(solution)/shard_map/ppermute | solution.py:40
  89.8 4.2 %collective-permute-done.27.refs_4_.carry_ref = bf16[256,256]{1,0:T(8,128)(2,1)S(1)} collective-permute-done((bf16[256,256]{1,0:T(8,128)(2,1)S(1)}, bf16[256,256]{1,0:T(8,128)(2,1)S(1)}, u32[]{:S(2)}, u32[]{:S(2)}) %collective-permute-start.27) | collective-permute-done | bytes 131104 | tf_op jit(solution)/shard_map/ppermute | solution.py:40
  94.1 2.7 %collective-permute-done.28.refs_5_.carry_ref = bf16[256,256]{1,0:T(8,128)(2,1)S(1)} collective-permute-done((bf16[256,256]{1,0:T(8,128)(2,1)S(1)}, bf16[256,256]{1,0:T(8,128)(2,1)S(1)}, u32[]{:S(2)}, u32[]{:S(2)}) %collective-permute-start.28) | collective-permute-done | bytes 131104 | tf_op jit(solution)/shard_map/ppermute | solution.py:40
  96.9 1.7 %collective-permute-start.34 = (bf16[2,256,512]{2,1,0:T(8,128)(2,1)S(1)}, bf16[2,256,512]{2,1,0:T(8,128)(2,1)S(1)}, u32[]{:S(2)}, u32[]{:S(2)}) collective-permute-start(bf16[2,256,512]{2,1,0:T(8,128)(2,1)S(1)} %copy-done.4), channel_id=1, source_target_pairs={{0,128},{1,129},{2,130},{3,131},{4,132},{5,133},{6,134},{7,135},{8... | collective-permute-start | bytes 1572872 | tf_op jit(solution)/shard_map/ppermute | solution.py:40
  101.0 11.7 %collective-permute-done.34.resident_ref = bf16[2,256,512]{2,1,0:T(8,128)(2,1)S(1)} collective-permute-done((bf16[2,256,512]{2,1,0:T(8,128)(2,1)S(1)}, bf16[2,256,512]{2,1,0:T(8,128)(2,1)S(1)}, u32[]{:S(2)}, u32[]{:S(2)}) %collective-permute-start.34) | collective-permute-done | bytes 524320 | tf_op jit(solution)/shard_map/ppermute | solution.py:40
  113.2 1.7 %collective-permute-start.35 = (bf16[2,256,256]{2,1,0:T(8,128)(2,1)S(1)}, bf16[2,256,256]{2,1,0:T(8,128)(2,1)S(1)}, u32[]{:S(2)}, u32[]{:S(2)}) collective-permute-start(bf16[2,256,256]{2,1,0:T(8,128)(2,1)S(1)} %shard_map.101), channel_id=1, source_target_pairs={{0,128},{1,129},{2,130},{3,131},{4,132},{5,133},{6,134},{7,135},{8... | collective-permute-start | bytes 786440 | tf_op jit(solution)/shard_map/ppermute | solution.py:40
  115.9 6.7 %collective-permute-done.35 = bf16[2,256,256]{2,1,0:T(8,128)(2,1)S(1)} collective-permute-done((bf16[2,256,256]{2,1,0:T(8,128)(2,1)S(1)}, bf16[2,256,256]{2,1,0:T(8,128)(2,1)S(1)}, u32[]{:S(2)}, u32[]{:S(2)}) %collective-permute-start.35) | collective-permute-done | bytes 262176 | tf_op jit(solution)/shard_map/ppermute | solution.py:40
  (95 shorter events, 31.5 us)
Async XLA Ops:
  1.7 9.7 %collective-permute-start.1 = (bf16[2,2,32,256]{3,2,1,0:T(8,128)(2,1)S(1)}, bf16[2,2,32,256]{3,2,1,0:T(8,128)(2,1)S(1)}, u32[]{:S(2)}, u32[]{:S(2)}) collective-permute-start(bf16[2,2,32,256]{3,2,1,0:T(8,128)(2,1)S(1)} %get-tuple-element.71), channel_id=1, source_target_pairs={{0,32},{1,33},{2,34},{3,35},{4,36},{5,37},{6,38},{7,39},{8,40},{9,... | collective-permute-start | bytes 196616 | tf_op jit(solution)/shard_map/ppermute | solution.py:40
  11.4 11.7 %collective-permute-start.2 = (bf16[2,2,2,32,256]{4,3,2,1,0:T(8,128)(2,1)S(1)}, bf16[2,2,2,32,256]{4,3,2,1,0:T(8,128)(2,1)S(1)}, u32[]{:S(2)}, u32[]{:S(2)}) collective-permute-start(bf16[2,2,2,32,256]{4,3,2,1,0:T(8,128)(2,1)S(1)} %shard_map.71.refs_0_), channel_id=1, source_target_pairs={{0,8},{1,65},{2,10},{3,67},{4,12},{5,69},{6,14},{7,71},{8,16},{9,7... | collective-permute-start | bytes 393224 | tf_op jit(solution)/shard_map/ppermute | solution.py:40
  13.1 10.0 %collective-permute-start.3 = (bf16[2,2,2,32,256]{4,3,2,1,0:T(8,128)(2,1)S(1)}, bf16[2,2,2,32,256]{4,3,2,1,0:T(8,128)(2,1)S(1)}, u32[]{:S(2)}, u32[]{:S(2)}) collective-permute-start(bf16[2,2,2,32,256]{4,3,2,1,0:T(8,128)(2,1)S(1)} %shard_map.71.refs_0_), channel_id=1, source_target_pairs={{0,24},{1,193},{2,26},{3,195},{4,28},{5,197},{6,30},{7,199},{8,0},... | collective-permute-start | bytes 393224 | tf_op jit(solution)/shard_map/ppermute | solution.py:40
  14.7 8.3 %collective-permute-start.4 = (bf16[2,2,2,32,256]{4,3,2,1,0:T(8,128)(2,1)S(1)}, bf16[2,2,2,32,256]{4,3,2,1,0:T(8,128)(2,1)S(1)}, u32[]{:S(2)}, u32[]{:S(2)}) collective-permute-start(bf16[2,2,2,32,256]{4,3,2,1,0:T(8,128)(2,1)S(1)} %shard_map.71.refs_0_), channel_id=1, source_target_pairs={{0,16},{1,129},{2,18},{3,131},{4,20},{5,133},{6,22},{7,135},{8,24}... | collective-permute-start | bytes 393224 | tf_op jit(solution)/shard_map/ppermute | solution.py:40
  16.7 9.1 %collective-permute-start.16 = (bf16[2,2,32,256]{3,2,1,0:T(8,128)(2,1)S(1)}, bf16[2,2,32,256]{3,2,1,0:T(8,128)(2,1)S(1)}, u32[]{:S(2)}, u32[]{:S(2)}) collective-permute-start(bf16[2,2,32,256]{3,2,1,0:T(8,128)(2,1)S(1)} %get-tuple-element.70), channel_id=1, source_target_pairs={{0,32},{1,33},{2,34},{3,35},{4,36},{5,37},{6,38},{7,39},{8,40},{9,... | collective-permute-start | bytes 196616 | tf_op jit(solution)/shard_map/ppermute | solution.py:40
  23.1 17.6 %collective-permute-start.5 = (bf16[4,1,2,2,32,256]{5,4,3,2,1,0:T(8,128)(2,1)S(1)}, bf16[4,1,2,2,32,256]{5,4,3,2,1,0:T(8,128)(2,1)S(1)}, u32[]{:S(2)}, u32[]{:S(2)}) collective-permute-start(bf16[4,1,2,2,32,256]{5,4,3,2,1,0:T(8,128)(2,1)S(1)} %shard_map.72.refs_0_), channel_id=1, source_target_pairs={{0,64},{1,9},{2,66},{3,11},{4,68},{5,13},{6,70},{7,15},{8,72},{9,1... | collective-permute-start | bytes 786440 | tf_op jit(solution)/shard_map/ppermute | solution.py:40
  25.8 11.5 %collective-permute-start.17 = (bf16[2,2,2,32,256]{4,3,2,1,0:T(8,128)(2,1)S(1)}, bf16[2,2,2,32,256]{4,3,2,1,0:T(8,128)(2,1)S(1)}, u32[]{:S(2)}, u32[]{:S(2)}) collective-permute-start(bf16[2,2,2,32,256]{4,3,2,1,0:T(8,128)(2,1)S(1)} %shard_map.82.refs_0_), channel_id=1, source_target_pairs={{0,8},{1,65},{2,10},{3,67},{4,12},{5,69},{6,14},{7,71},{8,16},{9,7... | collective-permute-start | bytes 393224 | tf_op jit(solution)/shard_map/ppermute | solution.py:40
  26.8 11.7 %collective-permute-start.18 = (bf16[2,2,2,32,256]{4,3,2,1,0:T(8,128)(2,1)S(1)}, bf16[2,2,2,32,256]{4,3,2,1,0:T(8,128)(2,1)S(1)}, u32[]{:S(2)}, u32[]{:S(2)}) collective-permute-start(bf16[2,2,2,32,256]{4,3,2,1,0:T(8,128)(2,1)S(1)} %shard_map.82.refs_0_), channel_id=1, source_target_pairs={{0,24},{1,193},{2,26},{3,195},{4,28},{5,197},{6,30},{7,199},{8,0},... | collective-permute-start | bytes 393224 | tf_op jit(solution)/shard_map/ppermute | solution.py:40
  29.1 11.5 %collective-permute-start.19 = (bf16[2,2,2,32,256]{4,3,2,1,0:T(8,128)(2,1)S(1)}, bf16[2,2,2,32,256]{4,3,2,1,0:T(8,128)(2,1)S(1)}, u32[]{:S(2)}, u32[]{:S(2)}) collective-permute-start(bf16[2,2,2,32,256]{4,3,2,1,0:T(8,128)(2,1)S(1)} %shard_map.82.refs_0_), channel_id=1, source_target_pairs={{0,16},{1,129},{2,18},{3,131},{4,20},{5,133},{6,22},{7,135},{8,24}... | collective-permute-start | bytes 393224 | tf_op jit(solution)/shard_map/ppermute | solution.py:40
  29.2 13.6 %collective-permute-start.6 = (bf16[4,1,2,2,32,256]{5,4,3,2,1,0:T(8,128)(2,1)S(1)}, bf16[4,1,2,2,32,256]{5,4,3,2,1,0:T(8,128)(2,1)S(1)}, u32[]{:S(2)}, u32[]{:S(2)}) collective-permute-start(bf16[4,1,2,2,32,256]{5,4,3,2,1,0:T(8,128)(2,1)S(1)} %shard_map.72.refs_0_), channel_id=1, source_target_pairs={{0,192},{1,25},{2,194},{3,27},{4,196},{5,29},{6,198},{7,31},{8,200... | collective-permute-start | bytes 786440 | tf_op jit(solution)/shard_map/ppermute | solution.py:40
  40.6 11.7 %collective-permute-start = (bf16[4,256,256]{2,1,0:T(8,128)(2,1)S(1)}, bf16[4,256,256]{2,1,0:T(8,128)(2,1)S(1)}, u32[]{:S(2)}, u32[]{:S(2)}) collective-permute-start(bf16[4,256,256]{2,1,0:T(8,128)(2,1)S(1)} %get-tuple-element.36.packed_ref), channel_id=1, source_target_pairs={{0,1},{1,0},{2,3},{3,2},{4,5},{5,4},{6,7},{7,6},{8,9},{9,8},{10,11... | collective-permute-start | bytes 1572872 | tf_op jit(solution)/shard_map/ppermute | solution.py:40
  42.8 24.0 %collective-permute-start.20 = (bf16[4,2,2,2,32,256]{5,4,3,2,1,0:T(8,128)(2,1)S(1)}, bf16[4,2,2,2,32,256]{5,4,3,2,1,0:T(8,128)(2,1)S(1)}, u32[]{:S(2)}, u32[]{:S(2)}) collective-permute-start(bf16[4,2,2,2,32,256]{5,4,3,2,1,0:T(8,128)(2,1)S(1)} %shard_map.83.refs_0_), channel_id=1, source_target_pairs={{0,64},{1,9},{2,66},{3,11},{4,68},{5,13},{6,70},{7,15},{8,72},{9,1... | collective-permute-start | bytes 1572872 | tf_op jit(solution)/shard_map/ppermute | solution.py:40
  45.2 22.8 %collective-permute-start.21 = (bf16[4,2,2,2,32,256]{5,4,3,2,1,0:T(8,128)(2,1)S(1)}, bf16[4,2,2,2,32,256]{5,4,3,2,1,0:T(8,128)(2,1)S(1)}, u32[]{:S(2)}, u32[]{:S(2)}) collective-permute-start(bf16[4,2,2,2,32,256]{5,4,3,2,1,0:T(8,128)(2,1)S(1)} %shard_map.83.refs_0_), channel_id=1, source_target_pairs={{0,192},{1,25},{2,194},{3,27},{4,196},{5,29},{6,198},{7,31},{8,200... | collective-permute-start | bytes 1572872 | tf_op jit(solution)/shard_map/ppermute | solution.py:40
  46.5 21.5 %collective-permute-start.22 = (bf16[4,2,2,2,32,256]{5,4,3,2,1,0:T(8,128)(2,1)S(1)}, bf16[4,2,2,2,32,256]{5,4,3,2,1,0:T(8,128)(2,1)S(1)}, u32[]{:S(2)}, u32[]{:S(2)}) collective-permute-start(bf16[4,2,2,2,32,256]{5,4,3,2,1,0:T(8,128)(2,1)S(1)} %shard_map.83.refs_0_), channel_id=1, source_target_pairs={{0,128},{1,17},{2,130},{3,19},{4,132},{5,21},{6,134},{7,23},{8,136... | collective-permute-start | bytes 1572872 | tf_op jit(solution)/shard_map/ppermute | solution.py:40
  48.0 15.5 %collective-permute-start.12 = (bf16[4,1,2,2,32,256]{5,4,3,2,1,0:T(8,128)(2,1)S(1)}, bf16[4,1,2,2,32,256]{5,4,3,2,1,0:T(8,128)(2,1)S(1)}, u32[]{:S(2)}, u32[]{:S(2)}) collective-permute-start(bf16[4,1,2,2,32,256]{5,4,3,2,1,0:T(8,128)(2,1)S(1)} %shard_map.76.refs_0_), channel_id=1, source_target_pairs={{0,128},{1,17},{2,130},{3,19},{4,132},{5,21},{6,134},{7,23},{8,136... | collective-permute-start | bytes 786440 | tf_op jit(solution)/shard_map/ppermute | solution.py:40
  52.3 17.4 %collective-permute-start.8 = (bf16[2,256,256]{2,1,0:T(8,128)(2,1)S(1)}, bf16[2,256,256]{2,1,0:T(8,128)(2,1)S(1)}, u32[]{:S(2)}, u32[]{:S(2)}) collective-permute-start(bf16[2,256,256]{2,1,0:T(8,128)(2,1)S(1)} %get-tuple-element.44), channel_id=1, source_target_pairs={{0,1},{1,0},{2,3},{3,2},{4,5},{5,4},{6,7},{7,6},{8,9},{9,8},{10,11... | collective-permute-start | bytes 786440 | tf_op jit(solution)/shard_map/ppermute | solution.py:40
  69.2 11.5 %collective-permute-start.23 = (bf16[2,256,256]{2,1,0:T(8,128)(2,1)S(1)}, bf16[2,256,256]{2,1,0:T(8,128)(2,1)S(1)}, u32[]{:S(2)}, u32[]{:S(2)}) collective-permute-start(bf16[2,256,256]{2,1,0:T(8,128)(2,1)S(1)} %get-tuple-element.56), channel_id=1, source_target_pairs={{0,1},{1,0},{2,3},{3,2},{4,5},{5,4},{6,7},{7,6},{8,9},{9,8},{10,11... | collective-permute-start | bytes 786440 | tf_op jit(solution)/shard_map/ppermute | solution.py:40
  74.9 14.3 %collective-permute-start.26 = (bf16[2,256,256]{2,1,0:T(8,128)(2,1)S(1)}, bf16[2,256,256]{2,1,0:T(8,128)(2,1)S(1)}, u32[]{:S(2)}, u32[]{:S(2)}) collective-permute-start(bf16[2,256,256]{2,1,0:T(8,128)(2,1)S(1)} %get-tuple-element.61), channel_id=1, source_target_pairs={{0,1},{1,0},{2,3},{3,2},{4,5},{5,4},{6,7},{7,6},{8,9},{9,8},{10,11... | collective-permute-start | bytes 786440 | tf_op jit(solution)/shard_map/ppermute | solution.py:40
  79.4 8.7 %collective-permute-start.25 = (bf16[256,256]{1,0:T(8,128)(2,1)S(1)}, bf16[256,256]{1,0:T(8,128)(2,1)S(1)}, u32[]{:S(2)}, u32[]{:S(2)}) collective-permute-start(bf16[256,256]{1,0:T(8,128)(2,1)S(1)} %shard_map.88), channel_id=1, source_target_pairs={{0,2},{1,3},{2,4},{3,5},{4,6},{5,7},{6,0},{7,1},{8,10},{9,11},{10,... | collective-permute-start | bytes 393224 | tf_op jit(solution)/shard_map/ppermute | solution.py:40
  85.7 8.2 %collective-permute-start.27 = (bf16[256,256]{1,0:T(8,128)(2,1)S(1)}, bf16[256,256]{1,0:T(8,128)(2,1)S(1)}, u32[]{:S(2)}, u32[]{:S(2)}) collective-permute-start(bf16[256,256]{1,0:T(8,128)(2,1)S(1)} %shard_map.92), channel_id=1, source_target_pairs={{0,2},{1,3},{2,4},{3,5},{4,6},{5,7},{6,0},{7,1},{8,10},{9,11},{10,... | collective-permute-start | bytes 393224 | tf_op jit(solution)/shard_map/ppermute | solution.py:40
  88.1 8.6 %collective-permute-start.28 = (bf16[256,256]{1,0:T(8,128)(2,1)S(1)}, bf16[256,256]{1,0:T(8,128)(2,1)S(1)}, u32[]{:S(2)}, u32[]{:S(2)}) collective-permute-start(bf16[256,256]{1,0:T(8,128)(2,1)S(1)} %shard_map.93), channel_id=1, source_target_pairs={{0,2},{1,3},{2,4},{3,5},{4,6},{5,7},{6,0},{7,1},{8,10},{9,11},{10,... | collective-permute-start | bytes 393224 | tf_op jit(solution)/shard_map/ppermute | solution.py:40
  96.9 15.8 %collective-permute-start.34 = (bf16[2,256,512]{2,1,0:T(8,128)(2,1)S(1)}, bf16[2,256,512]{2,1,0:T(8,128)(2,1)S(1)}, u32[]{:S(2)}, u32[]{:S(2)}) collective-permute-start(bf16[2,256,512]{2,1,0:T(8,128)(2,1)S(1)} %copy-done.4), channel_id=1, source_target_pairs={{0,128},{1,129},{2,130},{3,131},{4,132},{5,133},{6,134},{7,135},{8... | collective-permute-start | bytes 1572872 | tf_op jit(solution)/shard_map/ppermute | solution.py:40
  100.6 12.2 %collective-permute-start.33 = (bf16[2,256,256]{2,1,0:T(8,128)(2,1)S(1)}, bf16[2,256,256]{2,1,0:T(8,128)(2,1)S(1)}, u32[]{:S(2)}, u32[]{:S(2)}) collective-permute-start(bf16[2,256,256]{2,1,0:T(8,128)(2,1)S(1)} %get-tuple-element.69), channel_id=1, source_target_pairs={{0,1},{1,0},{2,3},{3,2},{4,5},{5,4},{6,7},{7,6},{8,9},{9,8},{10,11... | collective-permute-start | bytes 786440 | tf_op jit(solution)/shard_map/ppermute | solution.py:40
  113.2 9.3 %collective-permute-start.35 = (bf16[2,256,256]{2,1,0:T(8,128)(2,1)S(1)}, bf16[2,256,256]{2,1,0:T(8,128)(2,1)S(1)}, u32[]{:S(2)}, u32[]{:S(2)}) collective-permute-start(bf16[2,256,256]{2,1,0:T(8,128)(2,1)S(1)} %shard_map.101), channel_id=1, source_target_pairs={{0,128},{1,129},{2,130},{3,131},{4,132},{5,133},{6,134},{7,135},{8... | collective-permute-start | bytes 786440 | tf_op jit(solution)/shard_map/ppermute | solution.py:40
  (17 other events, 131.3 us)
where the time goes:
time: 123 us
  waiting for transfers between devices  59.8 us (49%)
  starting transfers between devices  44.6 us (36%)
  Pallas kernels  12.2 us (10%)
  local copies, waits for them, and re-layouts  4.65 us (4%)
    ppermute x36, waiting for transfers between devices, send(): return lax.ppermute(value, BOTH, pairs_of(move))  59.8 us
    ppermute x36, starting transfers between devices, send(): return lax.ppermute(value, BOTH, pairs_of(move))  44.6 us
    pallas_call x34, Pallas kernels, call(): pl.pallas_call(kernel, out_shape=outs, in_specs=specs, out_specs=jax.tree...  12.2 us
    unnamed x11, local copies, waits for them, and re-layouts  3.61 us
  transfers between devices with their start and end apart: 36, of which 17 were waited for; matrix products, arithmetic and copies ran while one was open for 1% of the time, Pallas kernels for 10%

commit v1 on v0

--- a/solution.py
+++ b/solution.py
@@ -169,11 +169,11 @@
     return lax.dot_general(left, right, (((0,), (0,)), ((), ())), preferred_element_type=F32)
 
 
-def put_history(tick, side, real_ref, imag_ref, past_ref, out_ref):
+def put_history(tick, side, unroll, real_ref, imag_ref, past_ref, out_ref):
     rows = slice(tick * TB, (tick + HW) * TB)
     at = pl.ds(pl.multiple_of(side * TB, TB), TB)
 
-    @pl.loop(0, 2)
+    @pl.loop(0, 2, unroll=unroll)
     def _(part):
         by_imag = turned(imag_ref[...], past_ref[1 - part, rows, at])
         by_imag = jnp.where(part == 0, -by_imag, by_imag)
@@ -181,7 +181,7 @@
 
 
 def keep_kernel(tick, real_ref, imag_ref, past_ref, out_ref):
-    put_history(tick, place()[4], real_ref, imag_ref, past_ref, out_ref)
+    put_history(tick, place()[4], False, real_ref, imag_ref, past_ref, out_ref)
 
 
 def history_kernel(tick, stacked, *refs):
@@ -198,7 +198,7 @@
                 real_ref[at, :] = sigma_refs[outer][inner, stacked, deep, 0]
                 imag_ref[at, :] = sigma_refs[outer][inner, stacked, deep, 1]
 
-    put_history(tick, 1 - core, real_ref, imag_ref, past_ref, give_ref)
+    put_history(tick, 1 - core, True, real_ref, imag_ref, past_ref, give_ref)
 
 
 def link_kernel(half, early, both_ref, carry_ref, base_ref, out_ref):

time: 123 us -> 122 us (level)
  transfers between devices with their start and end apart: 36 -> 36, of which waited for: 17 -> 18; matrix products, arithmetic and copies ran while one was open for 1% -> 1% of each run, Pallas kernels for 10% -> 9%
where the time goes in v1:
time: 122 us
  waiting for transfers between devices  60 us (49%)
  starting transfers between devices  44.6 us (37%)
  Pallas kernels  11 us (9%)
  local copies, waits for them, and re-layouts  4.65 us (4%)
    ppermute x36, waiting for transfers between devices, send(): return lax.ppermute(value, BOTH, pairs_of(move))  60 us
    ppermute x36, starting transfers between devices, send(): return lax.ppermute(value, BOTH, pairs_of(move))  44.6 us
    pallas_call x34, Pallas kernels, call(): pl.pallas_call(kernel, out_shape=outs, in_specs=specs, out_specs=jax.tree...  11 us
    unnamed x11, local copies, waits for them, and re-layouts  3.61 us
  transfers between devices with their start and end apart: 36, of which 18 were waited for; matrix products, arithmetic and copies ran while one was open for 1% of the time, Pallas kernels for 9%

profile of v1, /device:TPU:2, one launch (start us, length us, event | category | flops | bytes accessed | tf_op | source)
XLA Modules:
  0.0 122.3 jit_solution(16597681854948447620)
XLA Ops:
  1.7 7.3 %collective-permute-start.1 = (bf16[2,2,32,256]{3,2,1,0:T(8,128)(2,1)S(1)}, bf16[2,2,32,256]{3,2,1,0:T(8,128)(2,1)S(1)}, u32[]{:S(2)}, u32[]{:S(2)}) collective-permute-start(bf16[2,2,32,256]{3,2,1,0:T(8,128)(2,1)S(1)} %get-tuple-element.71), channel_id=1, source_target_pairs={{0,32},{1,33},{2,34},{3,35},{4,36},{5,37},{6,38},{7,39},{8,40},{9,... | collective-permute-start | bytes 196616 | tf_op jit(solution)/shard_map/ppermute | solution.py:40
  9.9 1.5 %collective-permute-done.1.theirs_ref = bf16[2,2,32,256]{3,2,1,0:T(8,128)(2,1)S(1)} collective-permute-done((bf16[2,2,32,256]{3,2,1,0:T(8,128)(2,1)S(1)}, bf16[2,2,32,256]{3,2,1,0:T(8,128)(2,1)S(1)}, u32[]{:S(2)}, u32[]{:S(2)}) %collective-permute-start.1) | collective-permute-done | bytes 65568 | tf_op jit(solution)/shard_map/ppermute | solution.py:40
  11.4 1.7 %collective-permute-start.2 = (bf16[2,2,2,32,256]{4,3,2,1,0:T(8,128)(2,1)S(1)}, bf16[2,2,2,32,256]{4,3,2,1,0:T(8,128)(2,1)S(1)}, u32[]{:S(2)}, u32[]{:S(2)}) collective-permute-start(bf16[2,2,2,32,256]{4,3,2,1,0:T(8,128)(2,1)S(1)} %shard_map.71.refs_0_), channel_id=1, source_target_pairs={{0,8},{1,65},{2,10},{3,67},{4,12},{5,69},{6,14},{7,71},{8,16},{9,7... | collective-permute-start | bytes 393224 | tf_op jit(solution)/shard_map/ppermute | solution.py:40
  13.1 1.7 %collective-permute-start.3 = (bf16[2,2,2,32,256]{4,3,2,1,0:T(8,128)(2,1)S(1)}, bf16[2,2,2,32,256]{4,3,2,1,0:T(8,128)(2,1)S(1)}, u32[]{:S(2)}, u32[]{:S(2)}) collective-permute-start(bf16[2,2,2,32,256]{4,3,2,1,0:T(8,128)(2,1)S(1)} %shard_map.71.refs_0_), channel_id=1, source_target_pairs={{0,24},{1,193},{2,26},{3,195},{4,28},{5,197},{6,30},{7,199},{8,0},... | collective-permute-start | bytes 393224 | tf_op jit(solution)/shard_map/ppermute | solution.py:40
  14.7 2.0 %collective-permute-start.4 = (bf16[2,2,2,32,256]{4,3,2,1,0:T(8,128)(2,1)S(1)}, bf16[2,2,2,32,256]{4,3,2,1,0:T(8,128)(2,1)S(1)}, u32[]{:S(2)}, u32[]{:S(2)}) collective-permute-start(bf16[2,2,2,32,256]{4,3,2,1,0:T(8,128)(2,1)S(1)} %shard_map.71.refs_0_), channel_id=1, source_target_pairs={{0,16},{1,129},{2,18},{3,131},{4,20},{5,133},{6,22},{7,135},{8,24}... | collective-permute-start | bytes 393224 | tf_op jit(solution)/shard_map/ppermute | solution.py:40
  16.7 6.4 %collective-permute-start.16 = (bf16[2,2,32,256]{3,2,1,0:T(8,128)(2,1)S(1)}, bf16[2,2,32,256]{3,2,1,0:T(8,128)(2,1)S(1)}, u32[]{:S(2)}, u32[]{:S(2)}) collective-permute-start(bf16[2,2,32,256]{3,2,1,0:T(8,128)(2,1)S(1)} %get-tuple-element.70), channel_id=1, source_target_pairs={{0,32},{1,33},{2,34},{3,35},{4,36},{5,37},{6,38},{7,39},{8,40},{9,... | collective-permute-start | bytes 196616 | tf_op jit(solution)/shard_map/ppermute | solution.py:40
  23.1 1.6 %collective-permute-start.5 = (bf16[4,1,2,2,32,256]{5,4,3,2,1,0:T(8,128)(2,1)S(1)}, bf16[4,1,2,2,32,256]{5,4,3,2,1,0:T(8,128)(2,1)S(1)}, u32[]{:S(2)}, u32[]{:S(2)}) collective-permute-start(bf16[4,1,2,2,32,256]{5,4,3,2,1,0:T(8,128)(2,1)S(1)} %shard_map.72.refs_0_), channel_id=1, source_target_pairs={{0,64},{1,9},{2,66},{3,11},{4,68},{5,13},{6,70},{7,15},{8,72},{9,1... | collective-permute-start | bytes 786440 | tf_op jit(solution)/shard_map/ppermute | solution.py:40
  26.8 2.3 %collective-permute-start.18 = (bf16[2,2,2,32,256]{4,3,2,1,0:T(8,128)(2,1)S(1)}, bf16[2,2,2,32,256]{4,3,2,1,0:T(8,128)(2,1)S(1)}, u32[]{:S(2)}, u32[]{:S(2)}) collective-permute-start(bf16[2,2,2,32,256]{4,3,2,1,0:T(8,128)(2,1)S(1)} %shard_map.82.refs_0_), channel_id=1, source_target_pairs={{0,24},{1,193},{2,26},{3,195},{4,28},{5,197},{6,30},{7,199},{8,0},... | collective-permute-start | bytes 393224 | tf_op jit(solution)/shard_map/ppermute | solution.py:40
  29.9 7.4 %collective-permute-done.17.refs_1_ = bf16[2,2,2,32,256]{4,3,2,1,0:T(8,128)(2,1)S(1)} collective-permute-done((bf16[2,2,2,32,256]{4,3,2,1,0:T(8,128)(2,1)S(1)}, bf16[2,2,2,32,256]{4,3,2,1,0:T(8,128)(2,1)S(1)}, u32[]{:S(2)}, u32[]{:S(2)}) %collective-permute-start.17) | collective-permute-done | bytes 131104 | tf_op jit(solution)/shard_map/ppermute | solution.py:40
  40.7 2.1 %collective-permute-start.11 = (bf16[4,1,2,2,32,256]{5,4,3,2,1,0:T(8,128)(2,1)S(1)}, bf16[4,1,2,2,32,256]{5,4,3,2,1,0:T(8,128)(2,1)S(1)}, u32[]{:S(2)}, u32[]{:S(2)}) collective-permute-start(bf16[4,1,2,2,32,256]{5,4,3,2,1,0:T(8,128)(2,1)S(1)} %shard_map.76.refs_0_), channel_id=1, source_target_pairs={{0,192},{1,25},{2,194},{3,27},{4,196},{5,29},{6,198},{7,31},{8,200... | collective-permute-start | bytes 786440 | tf_op jit(solution)/shard_map/ppermute | solution.py:40
  43.8 1.4 %collective-permute-done.7.refs_3_ = bf16[4,1,2,2,32,256]{5,4,3,2,1,0:T(8,128)(2,1)S(1)} collective-permute-done((bf16[4,1,2,2,32,256]{5,4,3,2,1,0:T(8,128)(2,1)S(1)}, bf16[4,1,2,2,32,256]{5,4,3,2,1,0:T(8,128)(2,1)S(1)}, u32[]{:S(2)}, u32[]{:S(2)}) %collective-permute-start.7) | collective-permute-done | bytes 262176 | tf_op jit(solution)/shard_map/ppermute | solution.py:40
  48.0 3.2 %collective-permute-start.12 = (bf16[4,1,2,2,32,256]{5,4,3,2,1,0:T(8,128)(2,1)S(1)}, bf16[4,1,2,2,32,256]{5,4,3,2,1,0:T(8,128)(2,1)S(1)}, u32[]{:S(2)}, u32[]{:S(2)}) collective-permute-start(bf16[4,1,2,2,32,256]{5,4,3,2,1,0:T(8,128)(2,1)S(1)} %shard_map.76.refs_0_), channel_id=1, source_target_pairs={{0,128},{1,17},{2,130},{3,19},{4,132},{5,21},{6,134},{7,23},{8,136... | collective-permute-start | bytes 786440 | tf_op jit(solution)/shard_map/ppermute | solution.py:40
  52.7 10.8 %collective-permute-done.12.refs_3_ = bf16[4,1,2,2,32,256]{5,4,3,2,1,0:T(8,128)(2,1)S(1)} collective-permute-done((bf16[4,1,2,2,32,256]{5,4,3,2,1,0:T(8,128)(2,1)S(1)}, bf16[4,1,2,2,32,256]{5,4,3,2,1,0:T(8,128)(2,1)S(1)}, u32[]{:S(2)}, u32[]{:S(2)}) %collective-permute-start.12) | collective-permute-done | bytes 262176 | tf_op jit(solution)/shard_map/ppermute | solution.py:40
  63.5 2.3 %collective-permute-start.9 = (bf16[2,256,256]{2,1,0:T(8,128)(2,1)S(1)}, bf16[2,256,256]{2,1,0:T(8,128)(2,1)S(1)}, u32[]{:S(2)}, u32[]{:S(2)}) collective-permute-start(bf16[2,256,256]{2,1,0:T(8,128)(2,1)S(1)} %get-tuple-element.47), channel_id=1, source_target_pairs={{0,2},{1,3},{2,0},{3,1},{4,5},{5,4},{6,7},{7,6},{8,10},{9,11},{10,... | collective-permute-start | bytes 786440 | tf_op jit(solution)/shard_map/ppermute | solution.py:40
  70.1 2.3 %collective-permute-start.14 = (bf16[256,256]{1,0:T(8,128)(2,1)S(1)}, bf16[256,256]{1,0:T(8,128)(2,1)S(1)}, u32[]{:S(2)}, u32[]{:S(2)}) collective-permute-start(bf16[256,256]{1,0:T(8,128)(2,1)S(1)} %shard_map.80), channel_id=1, source_target_pairs={{0,2},{1,3},{2,4},{3,5},{4,0},{5,1},{6,7},{7,6},{8,10},{9,11},{10,... | collective-permute-start | bytes 393224 | tf_op jit(solution)/shard_map/ppermute | solution.py:40
  75.3 2.2 %collective-permute-done.14.refs_4_.carry_ref = bf16[256,256]{1,0:T(8,128)(2,1)S(1)} collective-permute-done((bf16[256,256]{1,0:T(8,128)(2,1)S(1)}, bf16[256,256]{1,0:T(8,128)(2,1)S(1)}, u32[]{:S(2)}, u32[]{:S(2)}) %collective-permute-start.14) | collective-permute-done | bytes 131104 | tf_op jit(solution)/shard_map/ppermute | solution.py:40
  81.2 4.0 %collective-permute-done.24.refs_4_.carry_ref = bf16[256,256]{1,0:T(8,128)(2,1)S(1)} collective-permute-done((bf16[256,256]{1,0:T(8,128)(2,1)S(1)}, bf16[256,256]{1,0:T(8,128)(2,1)S(1)}, u32[]{:S(2)}, u32[]{:S(2)}) %collective-permute-start.24) | collective-permute-done | bytes 131104 | tf_op jit(solution)/shard_map/ppermute | solution.py:40
  85.3 1.8 %collective-permute-done.25.refs_5_.carry_ref = bf16[256,256]{1,0:T(8,128)(2,1)S(1)} collective-permute-done((bf16[256,256]{1,0:T(8,128)(2,1)S(1)}, bf16[256,256]{1,0:T(8,128)(2,1)S(1)}, u32[]{:S(2)}, u32[]{:S(2)}) %collective-permute-start.25) | collective-permute-done | bytes 131104 | tf_op jit(solution)/shard_map/ppermute | solution.py:40
  88.8 4.1 %collective-permute-done.27.refs_4_.carry_ref = bf16[256,256]{1,0:T(8,128)(2,1)S(1)} collective-permute-done((bf16[256,256]{1,0:T(8,128)(2,1)S(1)}, bf16[256,256]{1,0:T(8,128)(2,1)S(1)}, u32[]{:S(2)}, u32[]{:S(2)}) %collective-permute-start.27) | collective-permute-done | bytes 131104 | tf_op jit(solution)/shard_map/ppermute | solution.py:40
  93.1 2.7 %collective-permute-done.28.refs_5_.carry_ref = bf16[256,256]{1,0:T(8,128)(2,1)S(1)} collective-permute-done((bf16[256,256]{1,0:T(8,128)(2,1)S(1)}, bf16[256,256]{1,0:T(8,128)(2,1)S(1)}, u32[]{:S(2)}, u32[]{:S(2)}) %collective-permute-start.28) | collective-permute-done | bytes 131104 | tf_op jit(solution)/shard_map/ppermute | solution.py:40
  95.9 1.7 %collective-permute-start.34 = (bf16[2,256,512]{2,1,0:T(8,128)(2,1)S(1)}, bf16[2,256,512]{2,1,0:T(8,128)(2,1)S(1)}, u32[]{:S(2)}, u32[]{:S(2)}) collective-permute-start(bf16[2,256,512]{2,1,0:T(8,128)(2,1)S(1)} %copy-done.4), channel_id=1, source_target_pairs={{0,128},{1,129},{2,130},{3,131},{4,132},{5,133},{6,134},{7,135},{8... | collective-permute-start | bytes 1572872 | tf_op jit(solution)/shard_map/ppermute | solution.py:40
  100.0 11.7 %collective-permute-done.34.resident_ref = bf16[2,256,512]{2,1,0:T(8,128)(2,1)S(1)} collective-permute-done((bf16[2,256,512]{2,1,0:T(8,128)(2,1)S(1)}, bf16[2,256,512]{2,1,0:T(8,128)(2,1)S(1)}, u32[]{:S(2)}, u32[]{:S(2)}) %collective-permute-start.34) | collective-permute-done | bytes 524320 | tf_op jit(solution)/shard_map/ppermute | solution.py:40
  112.2 1.7 %collective-permute-start.35 = (bf16[2,256,256]{2,1,0:T(8,128)(2,1)S(1)}, bf16[2,256,256]{2,1,0:T(8,128)(2,1)S(1)}, u32[]{:S(2)}, u32[]{:S(2)}) collective-permute-start(bf16[2,256,256]{2,1,0:T(8,128)(2,1)S(1)} %shard_map.101), channel_id=1, source_target_pairs={{0,128},{1,129},{2,130},{3,131},{4,132},{5,133},{6,134},{7,135},{8... | collective-permute-start | bytes 786440 | tf_op jit(solution)/shard_map/ppermute | solution.py:40
  114.9 6.7 %collective-permute-done.35 = bf16[2,256,256]{2,1,0:T(8,128)(2,1)S(1)} collective-permute-done((bf16[2,256,256]{2,1,0:T(8,128)(2,1)S(1)}, bf16[2,256,256]{2,1,0:T(8,128)(2,1)S(1)}, u32[]{:S(2)}, u32[]{:S(2)}) %collective-permute-start.35) | collective-permute-done | bytes 262176 | tf_op jit(solution)/shard_map/ppermute | solution.py:40
  (95 shorter events, 30.8 us)
Async XLA Ops:
  1.7 9.7 %collective-permute-start.1 = (bf16[2,2,32,256]{3,2,1,0:T(8,128)(2,1)S(1)}, bf16[2,2,32,256]{3,2,1,0:T(8,128)(2,1)S(1)}, u32[]{:S(2)}, u32[]{:S(2)}) collective-permute-start(bf16[2,2,32,256]{3,2,1,0:T(8,128)(2,1)S(1)} %get-tuple-element.71), channel_id=1, source_target_pairs={{0,32},{1,33},{2,34},{3,35},{4,36},{5,37},{6,38},{7,39},{8,40},{9,... | collective-permute-start | bytes 196616 | tf_op jit(solution)/shard_map/ppermute | solution.py:40
  11.4 11.7 %collective-permute-start.2 = (bf16[2,2,2,32,256]{4,3,2,1,0:T(8,128)(2,1)S(1)}, bf16[2,2,2,32,256]{4,3,2,1,0:T(8,128)(2,1)S(1)}, u32[]{:S(2)}, u32[]{:S(2)}) collective-permute-start(bf16[2,2,2,32,256]{4,3,2,1,0:T(8,128)(2,1)S(1)} %shard_map.71.refs_0_), channel_id=1, source_target_pairs={{0,8},{1,65},{2,10},{3,67},{4,12},{5,69},{6,14},{7,71},{8,16},{9,7... | collective-permute-start | bytes 393224 | tf_op jit(solution)/shard_map/ppermute | solution.py:40
  13.1 10.0 %collective-permute-start.3 = (bf16[2,2,2,32,256]{4,3,2,1,0:T(8,128)(2,1)S(1)}, bf16[2,2,2,32,256]{4,3,2,1,0:T(8,128)(2,1)S(1)}, u32[]{:S(2)}, u32[]{:S(2)}) collective-permute-start(bf16[2,2,2,32,256]{4,3,2,1,0:T(8,128)(2,1)S(1)} %shard_map.71.refs_0_), channel_id=1, source_target_pairs={{0,24},{1,193},{2,26},{3,195},{4,28},{5,197},{6,30},{7,199},{8,0},... | collective-permute-start | bytes 393224 | tf_op jit(solution)/shard_map/ppermute | solution.py:40
  14.7 8.3 %collective-permute-start.4 = (bf16[2,2,2,32,256]{4,3,2,1,0:T(8,128)(2,1)S(1)}, bf16[2,2,2,32,256]{4,3,2,1,0:T(8,128)(2,1)S(1)}, u32[]{:S(2)}, u32[]{:S(2)}) collective-permute-start(bf16[2,2,2,32,256]{4,3,2,1,0:T(8,128)(2,1)S(1)} %shard_map.71.refs_0_), channel_id=1, source_target_pairs={{0,16},{1,129},{2,18},{3,131},{4,20},{5,133},{6,22},{7,135},{8,24}... | collective-permute-start | bytes 393224 | tf_op jit(solution)/shard_map/ppermute | solution.py:40
  16.7 9.1 %collective-permute-start.16 = (bf16[2,2,32,256]{3,2,1,0:T(8,128)(2,1)S(1)}, bf16[2,2,32,256]{3,2,1,0:T(8,128)(2,1)S(1)}, u32[]{:S(2)}, u32[]{:S(2)}) collective-permute-start(bf16[2,2,32,256]{3,2,1,0:T(8,128)(2,1)S(1)} %get-tuple-element.70), channel_id=1, source_target_pairs={{0,32},{1,33},{2,34},{3,35},{4,36},{5,37},{6,38},{7,39},{8,40},{9,... | collective-permute-start | bytes 196616 | tf_op jit(solution)/shard_map/ppermute | solution.py:40
  23.1 17.6 %collective-permute-start.5 = (bf16[4,1,2,2,32,256]{5,4,3,2,1,0:T(8,128)(2,1)S(1)}, bf16[4,1,2,2,32,256]{5,4,3,2,1,0:T(8,128)(2,1)S(1)}, u32[]{:S(2)}, u32[]{:S(2)}) collective-permute-start(bf16[4,1,2,2,32,256]{5,4,3,2,1,0:T(8,128)(2,1)S(1)} %shard_map.72.refs_0_), channel_id=1, source_target_pairs={{0,64},{1,9},{2,66},{3,11},{4,68},{5,13},{6,70},{7,15},{8,72},{9,1... | collective-permute-start | bytes 786440 | tf_op jit(solution)/shard_map/ppermute | solution.py:40
  25.8 11.5 %collective-permute-start.17 = (bf16[2,2,2,32,256]{4,3,2,1,0:T(8,128)(2,1)S(1)}, bf16[2,2,2,32,256]{4,3,2,1,0:T(8,128)(2,1)S(1)}, u32[]{:S(2)}, u32[]{:S(2)}) collective-permute-start(bf16[2,2,2,32,256]{4,3,2,1,0:T(8,128)(2,1)S(1)} %shard_map.82.refs_0_), channel_id=1, source_target_pairs={{0,8},{1,65},{2,10},{3,67},{4,12},{5,69},{6,14},{7,71},{8,16},{9,7... | collective-permute-start | bytes 393224 | tf_op jit(solution)/shard_map/ppermute | solution.py:40
  26.8 11.7 %collective-permute-start.18 = (bf16[2,2,2,32,256]{4,3,2,1,0:T(8,128)(2,1)S(1)}, bf16[2,2,2,32,256]{4,3,2,1,0:T(8,128)(2,1)S(1)}, u32[]{:S(2)}, u32[]{:S(2)}) collective-permute-start(bf16[2,2,2,32,256]{4,3,2,1,0:T(8,128)(2,1)S(1)} %shard_map.82.refs_0_), channel_id=1, source_target_pairs={{0,24},{1,193},{2,26},{3,195},{4,28},{5,197},{6,30},{7,199},{8,0},... | collective-permute-start | bytes 393224 | tf_op jit(solution)/shard_map/ppermute | solution.py:40
  29.1 11.5 %collective-permute-start.19 = (bf16[2,2,2,32,256]{4,3,2,1,0:T(8,128)(2,1)S(1)}, bf16[2,2,2,32,256]{4,3,2,1,0:T(8,128)(2,1)S(1)}, u32[]{:S(2)}, u32[]{:S(2)}) collective-permute-start(bf16[2,2,2,32,256]{4,3,2,1,0:T(8,128)(2,1)S(1)} %shard_map.82.refs_0_), channel_id=1, source_target_pairs={{0,16},{1,129},{2,18},{3,131},{4,20},{5,133},{6,22},{7,135},{8,24}... | collective-permute-start | bytes 393224 | tf_op jit(solution)/shard_map/ppermute | solution.py:40
  29.2 13.6 %collective-permute-start.6 = (bf16[4,1,2,2,32,256]{5,4,3,2,1,0:T(8,128)(2,1)S(1)}, bf16[4,1,2,2,32,256]{5,4,3,2,1,0:T(8,128)(2,1)S(1)}, u32[]{:S(2)}, u32[]{:S(2)}) collective-permute-start(bf16[4,1,2,2,32,256]{5,4,3,2,1,0:T(8,128)(2,1)S(1)} %shard_map.72.refs_0_), channel_id=1, source_target_pairs={{0,192},{1,25},{2,194},{3,27},{4,196},{5,29},{6,198},{7,31},{8,200... | collective-permute-start | bytes 786440 | tf_op jit(solution)/shard_map/ppermute | solution.py:40
  40.6 11.5 %collective-permute-start = (bf16[4,256,256]{2,1,0:T(8,128)(2,1)S(1)}, bf16[4,256,256]{2,1,0:T(8,128)(2,1)S(1)}, u32[]{:S(2)}, u32[]{:S(2)}) collective-permute-start(bf16[4,256,256]{2,1,0:T(8,128)(2,1)S(1)} %get-tuple-element.36.packed_ref), channel_id=1, source_target_pairs={{0,1},{1,0},{2,3},{3,2},{4,5},{5,4},{6,7},{7,6},{8,9},{9,8},{10,11... | collective-permute-start | bytes 1572872 | tf_op jit(solution)/shard_map/ppermute | solution.py:40
  42.8 23.8 %collective-permute-start.20 = (bf16[4,2,2,2,32,256]{5,4,3,2,1,0:T(8,128)(2,1)S(1)}, bf16[4,2,2,2,32,256]{5,4,3,2,1,0:T(8,128)(2,1)S(1)}, u32[]{:S(2)}, u32[]{:S(2)}) collective-permute-start(bf16[4,2,2,2,32,256]{5,4,3,2,1,0:T(8,128)(2,1)S(1)} %shard_map.83.refs_0_), channel_id=1, source_target_pairs={{0,64},{1,9},{2,66},{3,11},{4,68},{5,13},{6,70},{7,15},{8,72},{9,1... | collective-permute-start | bytes 1572872 | tf_op jit(solution)/shard_map/ppermute | solution.py:40
  45.2 22.6 %collective-permute-start.21 = (bf16[4,2,2,2,32,256]{5,4,3,2,1,0:T(8,128)(2,1)S(1)}, bf16[4,2,2,2,32,256]{5,4,3,2,1,0:T(8,128)(2,1)S(1)}, u32[]{:S(2)}, u32[]{:S(2)}) collective-permute-start(bf16[4,2,2,2,32,256]{5,4,3,2,1,0:T(8,128)(2,1)S(1)} %shard_map.83.refs_0_), channel_id=1, source_target_pairs={{0,192},{1,25},{2,194},{3,27},{4,196},{5,29},{6,198},{7,31},{8,200... | collective-permute-start | bytes 1572872 | tf_op jit(solution)/shard_map/ppermute | solution.py:40
  46.5 21.3 %collective-permute-start.22 = (bf16[4,2,2,2,32,256]{5,4,3,2,1,0:T(8,128)(2,1)S(1)}, bf16[4,2,2,2,32,256]{5,4,3,2,1,0:T(8,128)(2,1)S(1)}, u32[]{:S(2)}, u32[]{:S(2)}) collective-permute-start(bf16[4,2,2,2,32,256]{5,4,3,2,1,0:T(8,128)(2,1)S(1)} %shard_map.83.refs_0_), channel_id=1, source_target_pairs={{0,128},{1,17},{2,130},{3,19},{4,132},{5,21},{6,134},{7,23},{8,136... | collective-permute-start | bytes 1572872 | tf_op jit(solution)/shard_map/ppermute | solution.py:40
  48.0 15.5 %collective-permute-start.12 = (bf16[4,1,2,2,32,256]{5,4,3,2,1,0:T(8,128)(2,1)S(1)}, bf16[4,1,2,2,32,256]{5,4,3,2,1,0:T(8,128)(2,1)S(1)}, u32[]{:S(2)}, u32[]{:S(2)}) collective-permute-start(bf16[4,1,2,2,32,256]{5,4,3,2,1,0:T(8,128)(2,1)S(1)} %shard_map.76.refs_0_), channel_id=1, source_target_pairs={{0,128},{1,17},{2,130},{3,19},{4,132},{5,21},{6,134},{7,23},{8,136... | collective-permute-start | bytes 786440 | tf_op jit(solution)/shard_map/ppermute | solution.py:40
  52.1 17.1 %collective-permute-start.8 = (bf16[2,256,256]{2,1,0:T(8,128)(2,1)S(1)}, bf16[2,256,256]{2,1,0:T(8,128)(2,1)S(1)}, u32[]{:S(2)}, u32[]{:S(2)}) collective-permute-start(bf16[2,256,256]{2,1,0:T(8,128)(2,1)S(1)} %get-tuple-element.44), channel_id=1, source_target_pairs={{0,1},{1,0},{2,3},{3,2},{4,5},{5,4},{6,7},{7,6},{8,9},{9,8},{10,11... | collective-permute-start | bytes 786440 | tf_op jit(solution)/shard_map/ppermute | solution.py:40
  66.7 8.1 %collective-permute-start.13 = (bf16[2,256,256]{2,1,0:T(8,128)(2,1)S(1)}, bf16[2,256,256]{2,1,0:T(8,128)(2,1)S(1)}, u32[]{:S(2)}, u32[]{:S(2)}) collective-permute-start(bf16[2,256,256]{2,1,0:T(8,128)(2,1)S(1)} %get-tuple-element.50), channel_id=1, source_target_pairs={{0,1},{1,0},{2,3},{3,2},{4,5},{5,4},{6,7},{7,6},{8,9},{9,8},{10,11... | collective-permute-start | bytes 786440 | tf_op jit(solution)/shard_map/ppermute | solution.py:40
  68.7 11.9 %collective-permute-start.23 = (bf16[2,256,256]{2,1,0:T(8,128)(2,1)S(1)}, bf16[2,256,256]{2,1,0:T(8,128)(2,1)S(1)}, u32[]{:S(2)}, u32[]{:S(2)}) collective-permute-start(bf16[2,256,256]{2,1,0:T(8,128)(2,1)S(1)} %get-tuple-element.56), channel_id=1, source_target_pairs={{0,1},{1,0},{2,3},{3,2},{4,5},{5,4},{6,7},{7,6},{8,9},{9,8},{10,11... | collective-permute-start | bytes 786440 | tf_op jit(solution)/shard_map/ppermute | solution.py:40
  74.6 13.6 %collective-permute-start.26 = (bf16[2,256,256]{2,1,0:T(8,128)(2,1)S(1)}, bf16[2,256,256]{2,1,0:T(8,128)(2,1)S(1)}, u32[]{:S(2)}, u32[]{:S(2)}) collective-permute-start(bf16[2,256,256]{2,1,0:T(8,128)(2,1)S(1)} %get-tuple-element.61), channel_id=1, source_target_pairs={{0,1},{1,0},{2,3},{3,2},{4,5},{5,4},{6,7},{7,6},{8,9},{9,8},{10,11... | collective-permute-start | bytes 786440 | tf_op jit(solution)/shard_map/ppermute | solution.py:40
  78.9 8.2 %collective-permute-start.25 = (bf16[256,256]{1,0:T(8,128)(2,1)S(1)}, bf16[256,256]{1,0:T(8,128)(2,1)S(1)}, u32[]{:S(2)}, u32[]{:S(2)}) collective-permute-start(bf16[256,256]{1,0:T(8,128)(2,1)S(1)} %shard_map.88), channel_id=1, source_target_pairs={{0,2},{1,3},{2,4},{3,5},{4,6},{5,7},{6,0},{7,1},{8,10},{9,11},{10,... | collective-permute-start | bytes 393224 | tf_op jit(solution)/shard_map/ppermute | solution.py:40
  87.2 8.6 %collective-permute-start.28 = (bf16[256,256]{1,0:T(8,128)(2,1)S(1)}, bf16[256,256]{1,0:T(8,128)(2,1)S(1)}, u32[]{:S(2)}, u32[]{:S(2)}) collective-permute-start(bf16[256,256]{1,0:T(8,128)(2,1)S(1)} %shard_map.93), channel_id=1, source_target_pairs={{0,2},{1,3},{2,4},{3,5},{4,6},{5,7},{6,0},{7,1},{8,10},{9,11},{10,... | collective-permute-start | bytes 393224 | tf_op jit(solution)/shard_map/ppermute | solution.py:40
  95.9 15.8 %collective-permute-start.34 = (bf16[2,256,512]{2,1,0:T(8,128)(2,1)S(1)}, bf16[2,256,512]{2,1,0:T(8,128)(2,1)S(1)}, u32[]{:S(2)}, u32[]{:S(2)}) collective-permute-start(bf16[2,256,512]{2,1,0:T(8,128)(2,1)S(1)} %copy-done.4), channel_id=1, source_target_pairs={{0,128},{1,129},{2,130},{3,131},{4,132},{5,133},{6,134},{7,135},{8... | collective-permute-start | bytes 1572872 | tf_op jit(solution)/shard_map/ppermute | solution.py:40
  99.6 12.2 %collective-permute-start.33 = (bf16[2,256,256]{2,1,0:T(8,128)(2,1)S(1)}, bf16[2,256,256]{2,1,0:T(8,128)(2,1)S(1)}, u32[]{:S(2)}, u32[]{:S(2)}) collective-permute-start(bf16[2,256,256]{2,1,0:T(8,128)(2,1)S(1)} %get-tuple-element.69), channel_id=1, source_target_pairs={{0,1},{1,0},{2,3},{3,2},{4,5},{5,4},{6,7},{7,6},{8,9},{9,8},{10,11... | collective-permute-start | bytes 786440 | tf_op jit(solution)/shard_map/ppermute | solution.py:40
  112.2 9.3 %collective-permute-start.35 = (bf16[2,256,256]{2,1,0:T(8,128)(2,1)S(1)}, bf16[2,256,256]{2,1,0:T(8,128)(2,1)S(1)}, u32[]{:S(2)}, u32[]{:S(2)}) collective-permute-start(bf16[2,256,256]{2,1,0:T(8,128)(2,1)S(1)} %shard_map.101), channel_id=1, source_target_pairs={{0,128},{1,129},{2,130},{3,131},{4,132},{5,133},{6,134},{7,135},{8... | collective-permute-start | bytes 786440 | tf_op jit(solution)/shard_map/ppermute | solution.py:40
  (17 other events, 129.9 us)
